TPU v7x, 256 devices: a whole 4x4x8 slice. The times are simulated.
256 devices in a mesh: seq: 32 (over x, z), tp: 8 (over y, core).
Axes of the slice: x: 4, y: 4, z: 8, core: 2. Of those that a mesh axis runs over, the one named last changes fastest.
Arguments:
- tokens: bfloat16 [16384, 5376], P('seq'), may hold values from -6 to 6
- query_weight: bfloat16 [5376, 2048], P(None, 'tp')
- key_weight: bfloat16 [5376, 1024], P(None, 'tp')
- value_weight: bfloat16 [5376, 1024], P(None, 'tp'), may hold values from -0.078125 to 0.078125
- query_norm_gain: float32 [128], replicated, as said below
- key_norm_gain: float32 [128], replicated, as said below
- adapter_down_weight: bfloat16 [32, 5376, 64], P('seq', 'tp'), may hold values from -0.078125 to 0.078125
- adapter_up_weight: bfloat16 [32, 64, 2048], P('seq', None, 'tp'), may hold values from -0.75 to 0.75
- token_adapter_index: int32 [16384, 1], P('seq'), may hold values from 0 to 31; in each aligned block of 512 rows (0 to 511, 512 to 1023, ...) at most 32 rows name the same one
- packed_prompt_length: int32 [16], replicated, may hold values from 1 to 2048, 16384 in all
Outputs:
- attended: bfloat16 [16384, 2048], P('seq', 'tp')
Inputs may be any that keep to these rules, and one draw needn't show every extreme that they name: `token_adapter_index`: in each aligned block of 512 rows (the rows of one index of seq) no adapter is named by more than 32 rows, a bound that some block reaches. `packed_prompt_length`: they sum to 16384; the largest is exactly 2048. `query_norm_gain`: positive gains. `key_norm_gain`: positive gains.
All inputs are finite; a program needn't handle non-finite values.
Results may differ from a plain program's by a relative error of at most 0.02.
Values may be sent and summed in bfloat16 or wider, within the bound.
No kernel may reach another device: no remote copies, remote signals or barrier semaphores. Data moves between devices by JAX's collectives and lax.ppermute only.
A program may use at most 64 MiB of HBM per device.

v0:
```python
import jax
import jax.numpy as jnp
from jax import lax
from jax.sharding import PartitionSpec as P

WINDOW = 1024
query_scale = 0.07715167498104596


def passed_along(block, axis, distance):
    devices = range(lax.axis_size(axis))
    route = [(i - distance, i) for i in devices if i - distance in devices]
    return lax.ppermute(block, axis, route)


def make_dispatch(adapter_of, adapter_total, capacity):
    one_hot = (adapter_of[:, None] == jnp.arange(adapter_total, dtype=jnp.int32)[None, :]).astype(
        jnp.int32
    )
    before = jnp.cumsum(one_hot, axis=0) - one_hot
    slot_index = jnp.sum(before * one_hot, axis=1)
    target = adapter_of * capacity + slot_index
    return (
        jnp.arange(adapter_total * capacity, dtype=jnp.int32)[:, None] == target[None, :]
    ).astype(jnp.bfloat16)


def normalize(field, gain):
    return field / jnp.sqrt(jnp.mean(field * field, axis=-1, keepdims=True) + 1e-06) * gain


def rotate(field, positions):
    half = field.shape[-1] // 2
    freq = jnp.exp(
        -(2.0 * jnp.arange(half, dtype=jnp.float32) / field.shape[-1])
        * jnp.log(jnp.float32(10000.0))
    )
    angle = positions[:, None] * freq[None, :]
    cosine = jnp.cos(angle)[:, None, :]
    sine = jnp.sin(angle)[:, None, :]
    first = field[..., :half]
    second = field[..., half:]
    return jnp.concatenate(
        [first * cosine - second * sine, second * cosine + first * sine], axis=-1
    )


def body(
    tokens,
    query_weight,
    key_weight,
    value_weight,
    query_norm_gain,
    key_norm_gain,
    adapter_down_weight,
    adapter_up_weight,
    token_adapter_index,
    packed_prompt_length,
):
    rows = tokens.shape[0]
    head_dim = query_norm_gain.shape[0]
    kv_local = key_weight.shape[1] // head_dim
    q_local = query_weight.shape[1] // head_dim
    groups = q_local // kv_local
    seq_count = lax.axis_size("seq")
    owned_rows = adapter_down_weight.shape[0]
    adapter_total = owned_rows * seq_count
    capacity = 2 * rows // adapter_total
    feature_slice = adapter_down_weight.shape[1]
    seq_index = lax.axis_index("seq")
    tp_index = lax.axis_index("tp")
    dispatch = make_dispatch(token_adapter_index[:, 0], adapter_total, capacity)
    x_part = lax.dynamic_slice_in_dim(tokens, tp_index * feature_slice, feature_slice, 1)
    packed = jnp.dot(dispatch, x_part, preferred_element_type=jnp.float32).astype(jnp.bfloat16)
    down_all, up_all = (
        lax.all_gather(adapter_down_weight, "seq", axis=0, tiled=True),
        lax.all_gather(adapter_up_weight, "seq", axis=0, tiled=True),
    )
    packed = packed.reshape(adapter_total, capacity, feature_slice)
    partial_low = jnp.einsum("acd,adr->acr", packed, down_all, preferred_element_type=jnp.float32)
    low_rank = lax.psum(partial_low, "tp").astype(jnp.bfloat16)
    delta_slots = jnp.einsum(
        "acr,are->ace", low_rank, up_all, preferred_element_type=jnp.float32
    ).astype(jnp.bfloat16)
    delta_slots = delta_slots.reshape(adapter_total * capacity, q_local * head_dim)
    delta_rows = jnp.einsum("st,se->te", dispatch, delta_slots, preferred_element_type=jnp.float32)
    query = jnp.dot(tokens, query_weight, preferred_element_type=jnp.float32) + delta_rows
    keys = jnp.dot(tokens, key_weight, preferred_element_type=jnp.float32)
    values = jnp.dot(tokens, value_weight, preferred_element_type=jnp.float32).astype(jnp.bfloat16)
    positions = seq_index * rows + jnp.arange(rows, dtype=jnp.int32)
    pos_float = positions.astype(jnp.float32)
    query_rot = rotate(
        normalize(query.reshape(rows, q_local, head_dim), query_norm_gain), pos_float
    ).astype(jnp.bfloat16)
    key_rot = rotate(
        normalize(keys.reshape(rows, kv_local, head_dim), key_norm_gain), pos_float
    ).astype(jnp.bfloat16)
    reach = WINDOW // rows
    earlier = []
    for offset in range(reach, 0, -1):
        earlier.append(passed_along((key_rot, values), "seq", offset))
    all_keys = jnp.concatenate([piece[0] for piece in earlier] + [key_rot], axis=0)
    all_values = jnp.concatenate([piece[1] for piece in earlier] + [values], axis=0)
    all_values = all_values.reshape(WINDOW + rows, kv_local, head_dim)
    key_pos = seq_index * rows - WINDOW + jnp.arange(WINDOW + rows, dtype=jnp.int32)
    starts = jnp.cumsum(packed_prompt_length) - packed_prompt_length
    prompt_start = jnp.max(
        jnp.where(starts[None, :] <= positions[:, None], starts[None, :], 0), axis=1
    )
    lower = jnp.maximum(positions - WINDOW + 1, prompt_start)
    allowed = (key_pos[None, :] >= lower[:, None]) & (key_pos[None, :] <= positions[:, None])
    query_four = query_rot.reshape(rows, kv_local, groups, head_dim)
    scores = (
        jnp.einsum("tkgd,skd->kgts", query_four, all_keys, preferred_element_type=jnp.float32)
        * query_scale
    )
    scores = jnp.where(allowed[None, None], scores, jnp.float32(-1e30))
    peak = jnp.max(scores, axis=-1, keepdims=True)
    weights = jnp.exp(scores - peak)
    probs = (weights / jnp.sum(weights, axis=-1, keepdims=True)).astype(jnp.bfloat16)
    mixed = jnp.einsum("kgts,skd->tkgd", probs, all_values, preferred_element_type=jnp.float32)
    return mixed.astype(jnp.bfloat16).reshape(rows, q_local * head_dim)


def solution(mesh):
    in_specs = (
        P("seq", None),
        P(None, "tp"),
        P(None, "tp"),
        P(None, "tp"),
        P(),
        P(),
        P("seq", "tp", None),
        P("seq", None, "tp"),
        P("seq", None),
        P(),
    )
    out_specs = P("seq", "tp")
    return jax.shard_map(body, mesh=mesh, in_specs=in_specs, out_specs=out_specs, check_vma=False)
```

profile of v0, /device:TPU:8, one launch (start us, length us, event | category | flops | bytes accessed | tf_op | source)
XLA Modules:
  0.0 193.4 jit_solution(9777939212335164480)
XLA Ops:
  6.5 0.0 copy-start
  6.5 0.0 copy-start.5
  6.5 0.0 all-gather.3.cloned.1.call-start
  6.5 0.7 all-gather.3.cloned.1.call-update
  7.3 0.0 all-gather.5.cloned.1.call-start
  7.3 0.0 copy-start.1
  7.4 0.0 copy-start.8
  7.4 5.1 %multiply_reduce_fusion.1 = (f32[512]{0:T(512)S(1)}, f32[512,128]{0,1:T(8,128)S(1)}) fusion(bf16[512,5376]{1,0:T(8,128)(2,1)} %param.10, bf16[5376,128]{1,0:T(8,128)(2,1)} %param.12), kind=kOutput, calls=%fused_computation.43 | convolution fusion | flops 704773632 | bytes 7145472 | tf_op jit(solution)/shard_map/dot_general | solution.py:88
  12.4 0.0 copy-start.4
  12.4 0.0 copy-start.7
  12.5 0.0 copy-done.5
  12.5 0.1 multiply_bitcast_fusion
  12.6 0.6 fusion.34
  13.1 0.0 copy-start.2
  13.2 0.0 copy-start.3
  13.2 0.6 copy-done.2
  13.8 0.7 pad_maximum_fusion
  14.4 0.0 copy-done.3
  14.4 5.8 %collective-permute-start.2 = (bf16[512,1,128]{0,2,1:T(8,128)(2,1)}, bf16[512,1,128]{0,2,1:T(8,128)(2,1)}, u32[]{:S(2)}, u32[]{:S(2)}) collective-permute-start(bf16[512,1,128]{0,2,1:T(8,128)(2,1)} %pad_maximum_fusion), channel_id=1, source_target_pairs={{0,16},{8,24},{16,32},{24,40},{32,48},{40,56},{48,64},{56,72},{64,... | collective-permute-start | bytes 393224 | tf_op jit(solution)/shard_map/ppermute | solution.py:13
  20.2 4.5 %collective-permute-start.3 = (bf16[512,1,128]{0,2,1:T(8,128)(2,1)}, bf16[512,1,128]{0,2,1:T(8,128)(2,1)}, u32[]{:S(2)}, u32[]{:S(2)}) collective-permute-start(bf16[512,1,128]{0,2,1:T(8,128)(2,1)} %pad_maximum_fusion), channel_id=1, source_target_pairs={{0,8},{8,16},{16,24},{24,32},{32,40},{40,48},{48,56},{56,64},{64,7... | collective-permute-start | bytes 393224 | tf_op jit(solution)/shard_map/ppermute | solution.py:13
  24.7 0.0 copy-done.1
  24.7 0.0 copy-done.8
  24.7 2.2 %convolution_convert_fusion.1 = bf16[512,128]{1,0:T(8,128)(2,1)} fusion(bf16[512,5376]{1,0:T(8,128)(2,1)S(1)} %copy-done.1, bf16[5376,128]{1,0:T(8,128)(2,1)S(1)} %copy-done.8), kind=kOutput, calls=%fused_computation.15 | convolution fusion | flops 704708608 | bytes 7012352 | tf_op jit(solution)/shard_map/dot_general | solution.py:89
  27.0 4.9 %collective-permute-start = (bf16[512,128]{1,0:T(8,128)(2,1)}, bf16[512,128]{1,0:T(8,128)(2,1)}, u32[]{:S(2)}, u32[]{:S(2)}) collective-permute-start(bf16[512,128]{1,0:T(8,128)(2,1)} %convolution_convert_fusion.1), channel_id=1, source_target_pairs={{0,16},{8,24},{16,32},{24,40},{32,48},{40,56},{48,64},{56,72},{64,... | collective-permute-start | bytes 393224 | tf_op jit(solution)/shard_map/ppermute | solution.py:13
  31.8 3.6 %collective-permute-start.1 = (bf16[512,128]{1,0:T(8,128)(2,1)}, bf16[512,128]{1,0:T(8,128)(2,1)}, u32[]{:S(2)}, u32[]{:S(2)}) collective-permute-start(bf16[512,128]{1,0:T(8,128)(2,1)} %convolution_convert_fusion.1), channel_id=1, source_target_pairs={{0,8},{8,16},{16,24},{24,32},{32,40},{40,48},{48,56},{56,64},{64,7... | collective-permute-start | bytes 393224 | tf_op jit(solution)/shard_map/ppermute | solution.py:13
  35.4 0.0 all-gather.5.cloned.1.call-update
  35.4 0.0 copy-done.4
  35.5 1.2 reduce-window.20
  36.6 0.2 slice_reduce_fusion
  36.9 0.1 fusion.39
  37.0 0.0 copy-done.7
  37.0 0.1 copy.33
  37.1 0.1 reduce.4
  37.3 3.5 %fusion.6 = bf16[1024,672]{0,1:T(8,128)(2,1)} fusion(s32[512]{0:T(512)S(1)} %multiply_add_fusion, bf16[512,5376]{1,0:T(8,128)(2,1)} %param.10, s32[]{:T(128)S(6)} %select_n.12), kind=kOutput, calls=%fused_computation.11 | convolution fusion | flops 705855488 | bytes 2164740 | tf_op jit(solution)/shard_map/dot_general | solution.py:74
  40.8 0.1 select_reduce_fusion
  40.9 2.5 %copy.35 = bf16[1024,672]{1,0:T(8,128)(2,1)} copy(bf16[1024,672]{0,1:T(8,128)(2,1)} %fusion.6) | data formatting | bytes 2752512 | tf_op jit(solution)/shard_map/convert_element_type | solution.py:74
  43.5 1.8 multiply_cosine_fusion
  45.3 0.7 compare_and_fusion
  45.9 0.0 copy-done
  46.0 5.0 %fusion.47 = f32[512,256]{0,1:T(8,128)} fusion(bf16[512,5376]{1,0:T(8,128)(2,1)} %param.10, bf16[5376,256]{1,0:T(8,128)(2,1)S(1)} %copy-done), kind=kOutput, calls=%fused_computation.78 | convolution fusion | flops 1409286144 | bytes 8781824 | tf_op jit(solution)/shard_map/dot_general | solution.py:87
  51.0 0.0 copy-start.6
  51.0 41.4 %all-gather.3.cloned.1.call-done = bf16[32,672,64]{1,2,0:T(8,128)(2,1)} async-done(((bf16[1,672,64]{1,2,0:T(8,128)(2,1)}), bf16[32,672,64]{1,2,0:T(8,128)(2,1)}) %all-gather.3.cloned.1.call-update) | async-done | bytes 2752528 | tf_op jit(solution)/shard_map/all_gather | solution.py:76
  92.4 4.1 %fusion.48 = f32[32,32,64]{2,1,0:T(8,128)} fusion(bf16[32,32,672]{2,1,0:T(8,128)(2,1)} %bitcast.74, bf16[32,672,64]{1,2,0:T(8,128)(2,1)} %all-gather.3.cloned.1.call-done), kind=kOutput, calls=%fused_computation.79 | convolution fusion | flops 88080384 | bytes 4390912 | tf_op jit(solution)/shard_map/acd,adr->acr/dot_general | solution.py:80
  96.5 27.3 %all-reduce.1 = bf16[32,32,64]{2,1,0:T(8,128)(2,1)} all-reduce(f32[32,32,64]{2,1,0:T(8,128)} %fusion.48), channel_id=1, replica_groups=mesh['seq'=32,'tp'=8] {'tp'}, use_global_device_ids=true, to_apply=%region_6.7 | all-reduce | flops 65536 | bytes 393216 | tf_op jit(solution)/shard_map/psum | solution.py:81
  123.8 44.2 %all-gather.5.cloned.1.call-done = bf16[32,64,256]{2,1,0:T(8,128)(2,1)} async-done(((bf16[1,64,256]{2,1,0:T(8,128)(2,1)}), bf16[32,64,256]{2,1,0:T(8,128)(2,1)}) %all-gather.5.cloned.1.call-update) | async-done | bytes 1048592 | tf_op jit(solution)/shard_map/all_gather | solution.py:77
  167.9 1.6 convolution_convert_fusion
  169.6 2.5 %multiply_reduce_fusion = (f32[512,2]{0,1:T(2,128)S(1)}, f32[512,256]{0,1:T(8,128)}) fusion(f32[512,256]{0,1:T(8,128)} %fusion.47, bf16[1024,256]{1,0:T(8,128)(2,1)S(1)} %bitcast.75, s32[512]{0:T(512)S(1)} %multiply_add_fusion), kind=kOutput, calls=%fused_computation.22 | convolution fusion | flops 269351936 | bytes 1579008 | tf_op jit(solution)/shard_map/st,se->te/dot_general | solution.py:86
  172.0 2.0 %copy.36 = f32[512,2,128]{2,0,1:T(8,128)} copy(f32[512,2,128]{0,2,1:T(8,128)} %bitcast.76) | data formatting | bytes 1048576 | tf_op jit(solution)/shard_map/reshape | solution.py:93
  174.1 0.0 copy-done.6
  174.1 1.2 divide_multiply_fusion
  175.3 1.3 subtract_convert_fusion
  176.6 0.0 collective-permute-done.2
  176.6 0.0 collective-permute-done.3
  176.6 2.7 %fusion.1 = (f32[2,512]{1,0:T(2,128)S(1)}, f32[1536,512,2]{1,0,2:T(8,128)S(1)}) fusion(pred[512,1536]{0,1:T(8,128)(4,1)S(1)} %compare_and_fusion, bf16[512,2,64]{2,0,1:T(8,128)(2,1)S(1)} %get-tuple-element.6, bf16[512,2,64]{2,0,1:T(8,128)(2,1)S(1)} %get-tuple-element.5, bf16[512,1,64]{0,2,1:T(8,128)(2,1)} %copy-done.3, bf16[512,1,64]{0,2,1:T(8,128)(2,1)} %copy-done.2, ...), kind=kOutput, calls=%fused_computation.4 | convolution fusion | flops 409467904 | bytes 7737344 | tf_op jit(solution)/shard_map/tkgd,skd->kgts/dot_general | solution.py:114
  179.3 1.5 fusion
  180.8 0.0 collective-permute-done
  180.8 0.0 collective-permute-done.1
  180.8 3.9 %fusion.8 = bf16[128,2,512]{2,0,1:T(8,128)(2,1)} fusion(f32[2,512]{1,0:T(2,128)S(1)} %fusion, f32[2,512]{1,0:T(2,128)S(1)} %get-tuple-element.15, f32[1536,512,2]{1,0,2:T(8,128)S(1)} %get-tuple-element.16, pred[512,1536]{0,1:T(8,128)(4,1)S(1)} %compare_and_fusion, bf16[512,128]{1,0:T(8,128)(2,1)} %convolution_convert_fusion.1, ...), kind=kOutput, calls=%fused_computation.14 | convolution fusion | flops 411828224 | bytes 7741440 | tf_op jit(solution)/shard_map/kgts,skd->tkgd/dot_general | solution.py:121
  184.7 1.8 copy.40
  (13 shorter events, 0.1 us)
Async XLA Ops:
  6.5 39.4 %copy-start = (bf16[5376,256]{1,0:T(8,128)(2,1)S(1)}, bf16[5376,256]{1,0:T(8,128)(2,1)}, u32[]{:S(2)}) copy-start(bf16[5376,256]{1,0:T(8,128)(2,1)} %param.11) | copy-start | bytes 8257540
  6.5 5.9 %copy-start.5 = (f32[128]{0:T(128)S(1)}, f32[128]{0:T(128)}, u32[]{:S(2)}) copy-start(f32[128]{0:T(128)} %param.15) | copy-start | bytes 1540
  6.5 85.9 %all-gather.3.cloned.1.call-start = ((), (), s32[]{:S(2)}) async-start(), calls=%async_computation | async-start | bytes 3244032 | tf_op jit(solution)/shard_map/all_gather | solution.py:76
  7.3 160.7 %all-gather.5.cloned.1.call-start = ((), (), s32[]{:S(2)}) async-start(), calls=%async_computation.1 | async-start | bytes 1081344 | tf_op jit(solution)/shard_map/all_gather | solution.py:77
  7.3 17.4 %copy-start.1 = (bf16[512,5376]{1,0:T(8,128)(2,1)S(1)}, bf16[512,5376]{1,0:T(8,128)(2,1)}, u32[]{:S(2)}) copy-start(bf16[512,5376]{1,0:T(8,128)(2,1)} %param.10) | copy-start | bytes 16515076
  7.4 17.4 %copy-start.8 = (bf16[5376,128]{1,0:T(8,128)(2,1)S(1)}, bf16[5376,128]{1,0:T(8,128)(2,1)}, u32[]{:S(2)}) copy-start(bf16[5376,128]{1,0:T(8,128)(2,1)} %param.13) | copy-start | bytes 4128772
  12.4 23.0 %copy-start.4 = (s32[512,1]{0,1:T(1,128)S(1)}, s32[512,1]{0,1:T(1,128)}, u32[]{:S(2)}) copy-start(s32[512,1]{0,1:T(1,128)} %param.18) | copy-start | bytes 6148
  12.4 24.6 %copy-start.7 = (s32[16]{0:T(128)S(1)}, s32[16]{0:T(128)}, u32[]{:S(2)}) copy-start(s32[16]{0:T(128)} %param.19) | copy-start | bytes 196
  13.1 0.6 copy-start.2
  13.2 1.3 copy-start.3
  14.4 162.2 %collective-permute-start.2 = (bf16[512,1,128]{0,2,1:T(8,128)(2,1)}, bf16[512,1,128]{0,2,1:T(8,128)(2,1)}, u32[]{:S(2)}, u32[]{:S(2)}) collective-permute-start(bf16[512,1,128]{0,2,1:T(8,128)(2,1)} %pad_maximum_fusion), channel_id=1, source_target_pairs={{0,16},{8,24},{16,32},{24,40},{32,48},{40,56},{48,64},{56,72},{64,... | collective-permute-start | bytes 393224 | tf_op jit(solution)/shard_map/ppermute | solution.py:13
  20.2 156.4 %collective-permute-start.3 = (bf16[512,1,128]{0,2,1:T(8,128)(2,1)}, bf16[512,1,128]{0,2,1:T(8,128)(2,1)}, u32[]{:S(2)}, u32[]{:S(2)}) collective-permute-start(bf16[512,1,128]{0,2,1:T(8,128)(2,1)} %pad_maximum_fusion), channel_id=1, source_target_pairs={{0,8},{8,16},{16,24},{24,32},{32,40},{40,48},{48,56},{56,64},{64,7... | collective-permute-start | bytes 393224 | tf_op jit(solution)/shard_map/ppermute | solution.py:13
  27.0 153.8 %collective-permute-start = (bf16[512,128]{1,0:T(8,128)(2,1)}, bf16[512,128]{1,0:T(8,128)(2,1)}, u32[]{:S(2)}, u32[]{:S(2)}) collective-permute-start(bf16[512,128]{1,0:T(8,128)(2,1)} %convolution_convert_fusion.1), channel_id=1, source_target_pairs={{0,16},{8,24},{16,32},{24,40},{32,48},{40,56},{48,64},{56,72},{64,... | collective-permute-start | bytes 393224 | tf_op jit(solution)/shard_map/ppermute | solution.py:13
  31.8 149.0 %collective-permute-start.1 = (bf16[512,128]{1,0:T(8,128)(2,1)}, bf16[512,128]{1,0:T(8,128)(2,1)}, u32[]{:S(2)}, u32[]{:S(2)}) collective-permute-start(bf16[512,128]{1,0:T(8,128)(2,1)} %convolution_convert_fusion.1), channel_id=1, source_target_pairs={{0,8},{8,16},{16,24},{24,32},{32,40},{40,48},{48,56},{56,64},{64,7... | collective-permute-start | bytes 393224 | tf_op jit(solution)/shard_map/ppermute | solution.py:13
  51.0 123.1 %copy-start.6 = (f32[128]{0:T(128)S(1)}, f32[128]{0:T(128)}, u32[]{:S(2)}) copy-start(f32[128]{0:T(128)} %param.14) | copy-start | bytes 1540
Sparse Core Ops, SparseCore 0:
  9.9 82.4 all-gather.2
  95.0 72.9 all-gather.4
where the time goes:
time: 194 us; the launch traced here: 193 us
  waiting for transfers between devices  86.3 us (44%)
  matrix products  30.6 us (16%)
  blocking collectives  27.3 us (14%)
  starting transfers between devices  18.8 us (10%)
  between operations  13.6 us (7%)
  other arithmetic  9.43 us (5%)
  local copies, waits for them, and re-layouts  7.32 us (4%)
    all_gather x1, waiting for transfers between devices, body(): lax.all_gather(adapter_up_weight, 'seq', axis=0, tiled=True)  44.2 us
    all_gather x1, waiting for transfers between devices, body(): lax.all_gather(adapter_down_weight, 'seq', axis=0, tiled=True)  41.4 us
    psum x1, blocking collectives, body(): low_rank = lax.psum(partial_low, 'tp').astype(jnp.bfloat16)  27.3 us
    ppermute x4, starting transfers between devices, passed_along(): return lax.ppermute(block, axis, route)  18.7 us
    dot_general x1, matrix products, body(): keys = jnp.dot(tokens, key_weight, preferred_element_type=jnp.float32)  5.07 us
    dot_general x1, matrix products, body(): jnp.dot(tokens, query_weight, preferred_element_type=jnp.float32)  5.02 us
    dot_general x1, matrix products, body(): jnp.einsum('acd,adr->acr', packed, down_all, preferred_element_type=jnp.f...  4.11 us
    dot_general x1, matrix products, body(): jnp.einsum('kgts,skd->tkgd', probs, all_values, preferred_element_type=jn...  3.91 us
  transfers between devices with their start and end apart: 6, of which 2 were waited for; matrix products, arithmetic and copies ran while one was open for 21% of the time, Pallas kernels for 0%

commit v1 on v0

--- a/solution.py
+++ b/solution.py
@@ -78,7 +78,7 @@
     )
     packed = packed.reshape(adapter_total, capacity, feature_slice)
     partial_low = jnp.einsum("acd,adr->acr", packed, down_all, preferred_element_type=jnp.float32)
-    low_rank = lax.psum(partial_low, "tp").astype(jnp.bfloat16)
+    low_rank = jnp.sum(lax.all_gather(partial_low, "tp"), axis=0).astype(jnp.bfloat16)
     delta_slots = jnp.einsum(
         "acr,are->ace", low_rank, up_all, preferred_element_type=jnp.float32
     ).astype(jnp.bfloat16)

time: 194 us -> 232 us (1.20)
  waiting for transfers between devices: 86.3 us -> 148 us
  blocking collectives: 27.3 us -> 0 us
  other arithmetic: 9.43 us -> 15 us
  starting transfers between devices: 18.8 us -> 15 us
  matrix products: 30.6 us -> 33.6 us
    all_gather x1, waiting for transfers between devices: 41.4 us -> 75.2 us  [body(): lax.all_gather(adapter_down_weight, 'seq', axis=0, tiled=True)]
    all_gather x1, waiting for transfers between devices: 44.2 us -> 71.7 us  [body(): lax.all_gather(adapter_up_weight, 'seq', axis=0, tiled=True)]
    psum x1 -> x0, blocking collectives: 27.3 us -> none  [body(): low_rank = lax.psum(partial_low, 'tp').astype(jnp.bfloat16)]
    ppermute x4, starting transfers between devices: 18.7 us -> 14.9 us  [passed_along(): return lax.ppermute(block, axis, route)]
    reduce_sum x0 -> x1, other arithmetic: none -> 3.49 us  [body(): jnp.sum(lax.all_gather(partial_low, 'tp'), axis=0).astype(jnp.bfloat16)]
    dot_general x1, matrix products: 2.23 us -> 5.37 us  [body(): jnp.dot(tokens, value_weight, preferred_element_type=jnp.float32)]
  transfers between devices with their start and end apart: 6 -> 7, of which waited for: 2 -> 2; matrix products, arithmetic and copies ran while one was open for 21% -> 20% of each run, Pallas kernels for 0% -> 0%
where the time goes in v1:
time: 232 us
  waiting for transfers between devices  148 us (64%)
  matrix products  33.6 us (14%)
  starting transfers between devices  15 us (6%)
  other arithmetic  15 us (6%)
  between operations  13.3 us (6%)
  local copies, waits for them, and re-layouts  7.3 us (3%)
    all_gather x1, waiting for transfers between devices, body(): lax.all_gather(adapter_down_weight, 'seq', axis=0, tiled=True)  75.2 us
    all_gather x1, waiting for transfers between devices, body(): lax.all_gather(adapter_up_weight, 'seq', axis=0, tiled=True)  71.7 us
    ppermute x4, starting transfers between devices, passed_along(): return lax.ppermute(block, axis, route)  14.9 us
    dot_general x1, matrix products, body(): jnp.dot(tokens, value_weight, preferred_element_type=jnp.float32)  5.37 us
    dot_general x1, matrix products, body(): jnp.dot(tokens, query_weight, preferred_element_type=jnp.float32)  5 us
    dot_general x1, matrix products, body(): keys = jnp.dot(tokens, key_weight, preferred_element_type=jnp.float32)  4.92 us
  transfers between devices with their start and end apart: 7, of which 2 were waited for; matrix products, arithmetic and copies ran while one was open for 20% of the time, Pallas kernels for 0%

profile of v1, /device:TPU:8, one launch (start us, length us, event | category | flops | bytes accessed | tf_op | source)
XLA Modules:
  0.0 231.8 jit_solution(1550406330233095189)
XLA Ops:
  6.5 0.0 copy-start
  6.5 0.0 all-gather.5.cloned.1.call-start
  6.5 0.7 all-gather.5.cloned.1.call-update
  7.3 0.0 all-gather.9.cloned.1.call-start
  7.3 0.7 fusion.40
  8.1 1.2 reduce-window.20
  9.2 0.2 slice_reduce_fusion
  9.5 0.8 fusion.39
  10.3 0.7 multiply_add_fusion
  10.9 3.5 %fusion.6 = bf16[1024,672]{0,1:T(8,128)(2,1)} fusion(s32[512]{0:T(512)S(1)} %multiply_add_fusion, bf16[512,5376]{1,0:T(8,128)(2,1)} %param.10, s32[]{:T(128)S(6)} %select_n.12), kind=kOutput, calls=%fused_computation.11 | convolution fusion | flops 705855488 | bytes 2164740 | tf_op jit(solution)/shard_map/dot_general | solution.py:74
  14.5 2.5 %copy.36 = bf16[1024,672]{1,0:T(8,128)(2,1)} copy(bf16[1024,672]{0,1:T(8,128)(2,1)} %fusion.6) | data formatting | bytes 2752512 | tf_op jit(solution)/shard_map/convert_element_type | solution.py:74
  17.0 75.2 %all-gather.5.cloned.1.call-done = bf16[32,672,64]{1,2,0:T(8,128)(2,1)} async-done(((bf16[1,672,64]{1,2,0:T(8,128)(2,1)}), bf16[32,672,64]{1,2,0:T(8,128)(2,1)}) %all-gather.5.cloned.1.call-update) | async-done | bytes 2752528 | tf_op jit(solution)/shard_map/all_gather | solution.py:76
  92.2 4.1 %fusion.48 = f32[32,32,64]{2,1,0:T(8,128)} fusion(bf16[32,32,672]{2,1,0:T(8,128)(2,1)} %bitcast.75, bf16[32,672,64]{1,2,0:T(8,128)(2,1)} %all-gather.5.cloned.1.call-done), kind=kOutput, calls=%fused_computation.79 | convolution fusion | flops 88080384 | bytes 4390912 | tf_op jit(solution)/shard_map/acd,adr->acr/dot_general | solution.py:80
  96.3 0.0 copy-start.3
  96.3 0.0 all-gather.9.cloned.1.call-update
  96.4 0.0 all-gather.7.cloned.1.call-start
  96.4 4.9 %multiply_reduce_fusion.1 = (f32[512]{0:T(512)S(1)}, f32[512,128]{0,1:T(8,128)S(1)}) fusion(bf16[512,5376]{1,0:T(8,128)(2,1)} %param.10, bf16[5376,128]{1,0:T(8,128)(2,1)} %param.12), kind=kOutput, calls=%fused_computation.43 | convolution fusion | flops 704773632 | bytes 7145472 | tf_op jit(solution)/shard_map/dot_general | solution.py:88
  101.4 0.0 copy-start.5
  101.4 0.0 copy-done.3
  101.4 0.1 multiply_bitcast_fusion
  101.5 0.6 fusion.34
  102.1 0.0 copy-start.1
  102.1 0.0 copy-start.2
  102.1 0.6 copy-done.1
  102.7 0.7 pad_maximum_fusion
  103.3 0.0 copy-done.2
  103.3 3.9 %collective-permute-start.2 = (bf16[512,1,128]{0,2,1:T(8,128)(2,1)}, bf16[512,1,128]{0,2,1:T(8,128)(2,1)}, u32[]{:S(2)}, u32[]{:S(2)}) collective-permute-start(bf16[512,1,128]{0,2,1:T(8,128)(2,1)} %pad_maximum_fusion), channel_id=1, source_target_pairs={{0,16},{8,24},{16,32},{24,40},{32,48},{40,56},{48,64},{56,72},{64,... | collective-permute-start | bytes 393224 | tf_op jit(solution)/shard_map/ppermute | solution.py:13
  107.2 4.6 %collective-permute-start.3 = (bf16[512,1,128]{0,2,1:T(8,128)(2,1)}, bf16[512,1,128]{0,2,1:T(8,128)(2,1)}, u32[]{:S(2)}, u32[]{:S(2)}) collective-permute-start(bf16[512,1,128]{0,2,1:T(8,128)(2,1)} %pad_maximum_fusion), channel_id=1, source_target_pairs={{0,8},{8,16},{16,24},{24,32},{32,40},{40,48},{48,56},{56,64},{64,7... | collective-permute-start | bytes 393224 | tf_op jit(solution)/shard_map/ppermute | solution.py:13
  111.9 0.0 all-gather.7.cloned.1.call-update
  111.9 5.4 %convolution_convert_fusion.1 = bf16[512,128]{1,0:T(8,128)(2,1)} fusion(bf16[512,5376]{1,0:T(8,128)(2,1)} %param.10, bf16[5376,128]{1,0:T(8,128)(2,1)} %param.13), kind=kOutput, calls=%fused_computation.15 | convolution fusion | flops 704708608 | bytes 7012352 | tf_op jit(solution)/shard_map/dot_general | solution.py:89
  117.2 2.7 %collective-permute-start = (bf16[512,128]{1,0:T(8,128)(2,1)}, bf16[512,128]{1,0:T(8,128)(2,1)}, u32[]{:S(2)}, u32[]{:S(2)}) collective-permute-start(bf16[512,128]{1,0:T(8,128)(2,1)} %convolution_convert_fusion.1), channel_id=1, source_target_pairs={{0,16},{8,24},{16,32},{24,40},{32,48},{40,56},{48,64},{56,72},{64,... | collective-permute-start | bytes 393224 | tf_op jit(solution)/shard_map/ppermute | solution.py:13
  119.9 3.7 %collective-permute-start.1 = (bf16[512,128]{1,0:T(8,128)(2,1)}, bf16[512,128]{1,0:T(8,128)(2,1)}, u32[]{:S(2)}, u32[]{:S(2)}) collective-permute-start(bf16[512,128]{1,0:T(8,128)(2,1)} %convolution_convert_fusion.1), channel_id=1, source_target_pairs={{0,8},{8,16},{16,24},{24,32},{32,40},{40,48},{48,56},{56,64},{64,7... | collective-permute-start | bytes 393224 | tf_op jit(solution)/shard_map/ppermute | solution.py:13
  123.6 0.0 copy-done.5
  123.6 0.1 copy.34
  123.7 0.1 reduce.4
  123.9 0.1 select_reduce_fusion
  124.0 1.8 multiply_cosine_fusion
  125.8 0.7 compare_and_fusion
  126.5 0.0 copy-done
  126.5 5.0 %fusion.47 = f32[512,256]{0,1:T(8,128)} fusion(bf16[512,5376]{1,0:T(8,128)(2,1)} %param.10, bf16[5376,256]{1,0:T(8,128)(2,1)S(1)} %copy-done), kind=kOutput, calls=%fused_computation.78 | convolution fusion | flops 1409286144 | bytes 8781824 | tf_op jit(solution)/shard_map/dot_general | solution.py:87
  131.5 0.0 copy-start.4
  131.5 0.0 all-gather.9.cloned.1.call-done
  131.5 3.5 %reduce_sum.47 = bf16[32,32,64]{2,1,0:T(8,128)(2,1)} reduce(f32[8,32,32,64]{3,2,1,0:T(8,128)} %bitcast.76, f32[]{:T(128)} %constant.16.clone.1), dimensions={0}, to_apply=%region_6.7 | reduce | flops 458752 | bytes 2228228 | tf_op jit(solution)/shard_map/reduce_sum | solution.py:81
  135.0 71.7 %all-gather.7.cloned.1.call-done = bf16[32,64,256]{2,1,0:T(8,128)(2,1)} async-done(((bf16[1,64,256]{2,1,0:T(8,128)(2,1)}), bf16[32,64,256]{2,1,0:T(8,128)(2,1)}) %all-gather.7.cloned.1.call-update) | async-done | bytes 1048592 | tf_op jit(solution)/shard_map/all_gather | solution.py:77
  206.7 1.6 convolution_convert_fusion
  208.3 2.5 %multiply_reduce_fusion = (f32[512,2]{0,1:T(2,128)S(1)}, f32[512,256]{0,1:T(8,128)}) fusion(f32[512,256]{0,1:T(8,128)} %fusion.47, bf16[1024,256]{1,0:T(8,128)(2,1)S(1)} %bitcast.77, s32[512]{0:T(512)S(1)} %multiply_add_fusion), kind=kOutput, calls=%fused_computation.22 | convolution fusion | flops 269351936 | bytes 1579008 | tf_op jit(solution)/shard_map/st,se->te/dot_general | solution.py:86
  210.7 2.0 copy.37
  212.8 0.0 copy-done.4
  212.8 1.2 divide_multiply_fusion
  214.0 1.3 subtract_convert_fusion
  215.3 0.0 collective-permute-done.2
  215.3 0.0 collective-permute-done.3
  215.3 2.7 %fusion.1 = (f32[2,512]{1,0:T(2,128)S(1)}, f32[1536,512,2]{1,0,2:T(8,128)S(1)}) fusion(pred[512,1536]{0,1:T(8,128)(4,1)S(1)} %compare_and_fusion, bf16[512,2,64]{2,0,1:T(8,128)(2,1)S(1)} %get-tuple-element.6, bf16[512,2,64]{2,0,1:T(8,128)(2,1)S(1)} %get-tuple-element.5, bf16[512,1,64]{0,2,1:T(8,128)(2,1)} %copy-done.2, bf16[512,1,64]{0,2,1:T(8,128)(2,1)} %copy-done.1, ...), kind=kOutput, calls=%fused_computation.4 | convolution fusion | flops 409467904 | bytes 7737344 | tf_op jit(solution)/shard_map/tkgd,skd->kgts/dot_general | solution.py:114
  218.0 1.5 fusion
  219.5 0.0 collective-permute-done
  219.5 0.0 collective-permute-done.1
  219.5 3.9 %fusion.8 = bf16[128,2,512]{2,0,1:T(8,128)(2,1)} fusion(f32[2,512]{1,0:T(2,128)S(1)} %fusion, f32[2,512]{1,0:T(2,128)S(1)} %get-tuple-element.15, f32[1536,512,2]{1,0,2:T(8,128)S(1)} %get-tuple-element.16, pred[512,1536]{0,1:T(8,128)(4,1)S(1)} %compare_and_fusion, bf16[512,128]{1,0:T(8,128)(2,1)} %convolution_convert_fusion.1, ...), kind=kOutput, calls=%fused_computation.14 | convolution fusion | flops 411828224 | bytes 7741440 | tf_op jit(solution)/shard_map/kgts,skd->tkgd/dot_general | solution.py:121
  223.4 1.8 copy.41
  (11 shorter events, 0.1 us)
Async XLA Ops:
  6.5 119.9 %copy-start = (bf16[5376,256]{1,0:T(8,128)(2,1)S(1)}, bf16[5376,256]{1,0:T(8,128)(2,1)}, u32[]{:S(2)}) copy-start(bf16[5376,256]{1,0:T(8,128)(2,1)} %param.11) | copy-start | bytes 8257540
  6.5 85.7 %all-gather.5.cloned.1.call-start = ((), (), s32[]{:S(2)}) async-start(), calls=%async_computation | async-start | bytes 3244032 | tf_op jit(solution)/shard_map/all_gather | solution.py:76
  7.3 124.2 %all-gather.9.cloned.1.call-start = ((), (), s32[]{:S(2)}) async-start(), calls=%async_computation.2 | async-start | bytes 4718592 | tf_op jit(solution)/shard_map/all_gather | solution.py:81
  96.3 5.1 %copy-start.3 = (f32[128]{0:T(128)S(1)}, f32[128]{0:T(128)}, u32[]{:S(2)}) copy-start(f32[128]{0:T(128)} %param.15) | copy-start | bytes 1540
  96.4 110.3 %all-gather.7.cloned.1.call-start = ((), (), s32[]{:S(2)}) async-start(), calls=%async_computation.1 | async-start | bytes 1081344 | tf_op jit(solution)/shard_map/all_gather | solution.py:77
  101.4 22.2 %copy-start.5 = (s32[16]{0:T(128)S(1)}, s32[16]{0:T(128)}, u32[]{:S(2)}) copy-start(s32[16]{0:T(128)} %param.19) | copy-start | bytes 196
  102.1 0.6 copy-start.1
  102.1 1.3 copy-start.2
  103.3 112.0 %collective-permute-start.2 = (bf16[512,1,128]{0,2,1:T(8,128)(2,1)}, bf16[512,1,128]{0,2,1:T(8,128)(2,1)}, u32[]{:S(2)}, u32[]{:S(2)}) collective-permute-start(bf16[512,1,128]{0,2,1:T(8,128)(2,1)} %pad_maximum_fusion), channel_id=1, source_target_pairs={{0,16},{8,24},{16,32},{24,40},{32,48},{40,56},{48,64},{56,72},{64,... | collective-permute-start | bytes 393224 | tf_op jit(solution)/shard_map/ppermute | solution.py:13
  107.2 108.1 %collective-permute-start.3 = (bf16[512,1,128]{0,2,1:T(8,128)(2,1)}, bf16[512,1,128]{0,2,1:T(8,128)(2,1)}, u32[]{:S(2)}, u32[]{:S(2)}) collective-permute-start(bf16[512,1,128]{0,2,1:T(8,128)(2,1)} %pad_maximum_fusion), channel_id=1, source_target_pairs={{0,8},{8,16},{16,24},{24,32},{32,40},{40,48},{48,56},{56,64},{64,7... | collective-permute-start | bytes 393224 | tf_op jit(solution)/shard_map/ppermute | solution.py:13
  117.2 102.3 %collective-permute-start = (bf16[512,128]{1,0:T(8,128)(2,1)}, bf16[512,128]{1,0:T(8,128)(2,1)}, u32[]{:S(2)}, u32[]{:S(2)}) collective-permute-start(bf16[512,128]{1,0:T(8,128)(2,1)} %convolution_convert_fusion.1), channel_id=1, source_target_pairs={{0,16},{8,24},{16,32},{24,40},{32,48},{40,56},{48,64},{56,72},{64,... | collective-permute-start | bytes 393224 | tf_op jit(solution)/shard_map/ppermute | solution.py:13
  119.9 99.6 %collective-permute-start.1 = (bf16[512,128]{1,0:T(8,128)(2,1)}, bf16[512,128]{1,0:T(8,128)(2,1)}, u32[]{:S(2)}, u32[]{:S(2)}) collective-permute-start(bf16[512,128]{1,0:T(8,128)(2,1)} %convolution_convert_fusion.1), channel_id=1, source_target_pairs={{0,8},{8,16},{16,24},{24,32},{32,40},{40,48},{48,56},{56,64},{64,7... | collective-permute-start | bytes 393224 | tf_op jit(solution)/shard_map/ppermute | solution.py:13
  131.5 81.3 %copy-start.4 = (f32[128]{0:T(128)S(1)}, f32[128]{0:T(128)}, u32[]{:S(2)}) copy-start(f32[128]{0:T(128)} %param.14) | copy-start | bytes 1540
Sparse Core Ops, SparseCore 0:
  9.9 82.2 all-gather.4
  96.5 30.2 all-gather.8
  129.3 77.2 all-gather.6
